TPU v7x, 128 devices: a whole 4x4x4 slice. The times are simulated.
128 devices in a mesh: corpus: 4 (over x), blk: 32 (over z, y, core).
Axes of the slice: x: 4, y: 4, z: 4, core: 2. Of those that a mesh axis runs over, the one named last changes fastest.
Arguments:
- embedding: bfloat16 [32768, 1024], P(('corpus', 'blk'))
- cluster: int32 [32768], P(('corpus', 'blk')), may hold values from 0 to 7, as said below
- order: int32 [32768], P(('corpus', 'blk')), may hold values from 0 to 32767, each once
Outputs:
- nearest: float32 [32768], P(('corpus', 'blk'))
Inputs may be any that keep to these rules, and one draw needn't show every extreme that they name: On every device, at most 128 documents have clusters with any one value of cluster mod 4. All devices with the same blk index have one common value that exactly 128 of their documents take. `order`: each number appears once.
All inputs are finite; a program needn't handle non-finite values.
Results may differ from a plain program's by a relative error of at most 0.0013.
Values may be sent and summed in bfloat16 or wider, within the bound.
No kernel may reach another device: no remote copies, remote signals or barrier semaphores. Data moves between devices by JAX's collectives and lax.ppermute only.
A program may use at most 128 MiB of HBM per device.

v0:
```python
import jax
import jax.numpy as jnp
from jax import lax
from jax.sharding import PartitionSpec as P


def normalize(values):
    wide = values.astype(jnp.float32)
    return (wide * lax.rsqrt(jnp.sum(wide * wide, axis=1, keepdims=True) + 1e-06)).astype(
        jnp.bfloat16
    )


def similarity(left, right):
    return lax.dot_general(
        left, right, (((1,), (1,)), ((), ())), preferred_element_type=jnp.float32
    )


def local(embedding, cluster, order):
    groups = lax.axis_size("corpus")
    capacity = embedding.shape[0] // 2
    count = groups * capacity
    unit = normalize(embedding)
    target = jnp.mod(cluster, groups)
    picks = (target[:, None] == jnp.arange(groups, dtype=jnp.int32)[None, :]).astype(jnp.int32)
    ranks = jnp.cumsum(picks, axis=0) - 1
    place = target * capacity + jnp.sum(picks * ranks, axis=1)
    send_vecs = jnp.zeros((count, unit.shape[1]), jnp.bfloat16).at[place].set(unit)
    send_keys = jnp.full((count,), -1, jnp.int32).at[place].set(cluster)
    send_order = jnp.zeros((count,), jnp.int32).at[place].set(order)
    got_vecs, got_keys, got_order = (
        lax.all_to_all(
            send_vecs.reshape(groups, capacity, -1),
            "corpus",
            split_axis=0,
            concat_axis=0,
            tiled=True,
        ),
        lax.all_to_all(
            send_keys.reshape(groups, capacity), "corpus", split_axis=0, concat_axis=0, tiled=True
        ),
        lax.all_to_all(
            send_order.reshape(groups, capacity), "corpus", split_axis=0, concat_axis=0, tiled=True
        ),
    )
    vecs = got_vecs.reshape(count, -1)
    keys = got_keys.reshape(count)
    ranks_recv = got_order.reshape(count)
    lowest = jnp.full((count,), -1.0, jnp.float32)
    other_vecs = lax.all_gather(vecs, "blk", axis=0, tiled=True)
    other_keys = lax.all_gather(keys, "blk", axis=0, tiled=True)
    other_order = lax.all_gather(ranks_recv, "blk", axis=0, tiled=True)
    sims = similarity(vecs, other_vecs)
    keep = (
        (keys[:, None] == other_keys[None, :])
        & (keys[:, None] >= 0)
        & (other_order[None, :] < ranks_recv[:, None])
    )
    best = jnp.maximum(lowest, jnp.max(jnp.where(keep, sims, jnp.float32(-1.0)), axis=1))
    back = lax.all_to_all(
        best.reshape(groups, capacity), "corpus", split_axis=0, concat_axis=0, tiled=True
    )
    return back.reshape(-1)[place]


def solution(mesh):
    in_specs = (P(("corpus", "blk"), None), P(("corpus", "blk")), P(("corpus", "blk")))
    out_specs = P(("corpus", "blk"))
    return jax.shard_map(local, mesh=mesh, in_specs=in_specs, out_specs=out_specs, check_vma=False)
```

profile of v0, /device:TPU:0, one launch (start us, length us, event | category | flops | bytes accessed | tf_op | source)
XLA Modules:
  0.0 194.6 jit_solution(5818480411853797685)
XLA Ops:
  6.5 0.0 all-gather.4.cloned.1.call-start
  6.5 0.7 fusion.15
  7.2 0.7 and_select_fusion
  7.9 1.2 reduce-window.6
  9.1 0.1 slice.10
  9.2 0.1 copy.10
  9.4 0.1 copy.11
  9.5 0.1 add_bitcast_fusion
  9.6 0.7 compare_select_fusion
  10.3 1.2 fusion
  11.5 2.5 %scatter_custom_fusion.2 = bf16[512,1024]{1,0:T(8,128)(2,1)S(1)} fusion(s32[256]{0:T(256)S(1)} %compare_select_fusion, bf16[256,1024]{1,0:T(8,128)(2,1)} %param.3, f32[256]{0:T(256)S(1)} %add_rsqrt_fusion, bf16[]{:T(256)} %constant.21.clone.1), kind=kCustom, calls=%fused_computation.9 | custom fusion | flops 786432 | bytes 1573890 | tf_op jit(solution)/shard_map/scatter | solution.py:29
  14.0 19.4 %all_to_all.29 = bf16[4,128,1024]{2,1,0:T(8,128)(2,1)} all-to-all(bf16[4,128,1024]{2,1,0:T(8,128)(2,1)S(1)} %bitcast.34), channel_id=1, replica_groups=mesh['corpus'=4,'blk'=32] {'corpus'}, dimensions={0} | all-to-all | bytes 2097152 | tf_op jit(solution)/shard_map/all_to_all | solution.py:33
  33.4 0.0 all-gather.4.cloned.1.call-update
  33.4 2.1 %scatter_custom_fusion = s32[512]{0:T(512)} fusion(s32[256]{0:T(256)S(1)} %compare_select_fusion, s32[256]{0:T(256)} %param.4, s32[]{:T(128)} %constant.12.clone.1), kind=kCustom, calls=%fused_computation.29 | custom fusion | bytes 2560 | tf_op jit(solution)/shard_map/scatter | solution.py:30
  35.5 3.2 %all-to-all-start = ((s32[4,1,128]{2,1,0:T(1,128)}), s32[4,1,128]{2,1,0:T(1,128)S(1)}, u32[]{:S(2)}, u32[]{:S(2)}) async-start(s32[4,1,128]{2,1,0:T(1,128)} %bitcast.3), calls=%async_computation | async-start | bytes 4096 | tf_op jit(solution)/shard_map/all_to_all | solution.py:40
  38.6 2.1 %scatter_custom_fusion.1 = s32[512]{0:T(512)} fusion(s32[256]{0:T(256)S(1)} %compare_select_fusion, s32[256]{0:T(256)} %param.5, s32[]{:T(128)} %constant.13.clone.1), kind=kCustom, calls=%fused_computation.26 | custom fusion | bytes 2560 | tf_op jit(solution)/shard_map/scatter | solution.py:31
  40.7 3.2 %all-to-all-done = s32[4,1,128]{2,1,0:T(1,128)S(1)} async-done(((s32[4,1,128]{2,1,0:T(1,128)}), s32[4,1,128]{2,1,0:T(1,128)S(1)}, u32[]{:S(2)}, u32[]{:S(2)}) %all-to-all-start) | async-done | bytes 2080 | tf_op jit(solution)/shard_map/all_to_all | solution.py:40
  43.9 3.2 %all-to-all-start.1 = ((s32[4,1,128]{2,1,0:T(1,128)}), s32[4,1,128]{2,1,0:T(1,128)S(1)}, u32[]{:S(2)}, u32[]{:S(2)}) async-start(s32[4,1,128]{2,1,0:T(1,128)} %bitcast.7), calls=%async_computation.1 | async-start | bytes 4096 | tf_op jit(solution)/shard_map/all_to_all | solution.py:43
  47.1 26.2 %all-gather = s32[32,1,512]{2,1,0:T(1,128)S(1)} all-gather(s32[1,1,512]{2,1,0:T(1,128)S(1)} %bitcast.37), channel_id=1, replica_groups=mesh['corpus'=4,'blk'=32] {'blk'}, dimensions={0}, use_global_device_ids=true | all-gather | bytes 67584 | tf_op jit(solution)/shard_map/all_gather | solution.py:52
  73.3 0.0 all-to-all-done.1
  73.3 24.5 %all-gather.1 = s32[32,1,512]{2,1,0:T(1,128)S(1)} all-gather(s32[1,1,512]{2,1,0:T(1,128)S(1)} %bitcast.40), channel_id=1, replica_groups=mesh['corpus'=4,'blk'=32] {'blk'}, dimensions={0}, use_global_device_ids=true | all-gather | bytes 67584 | tf_op jit(solution)/shard_map/all_gather | solution.py:53
  97.9 50.3 %all-gather.4.cloned.1.call-done = bf16[16384,1024]{1,0:T(8,128)(2,1)} async-done(((bf16[512,1024]{1,0:T(8,128)(2,1)}), bf16[16384,1024]{1,0:T(8,128)(2,1)}) %all-gather.4.cloned.1.call-update) | async-done | bytes 33554448 | tf_op jit(solution)/shard_map/all_gather | solution.py:51
  148.1 27.1 %select_reduce_fusion = f32[512]{0:T(512)S(1)} fusion(bf16[512,1024]{1,0:T(8,128)(2,1)} %bitcast.33, bf16[16384,1024]{1,0:T(8,128)(2,1)} %all-gather.4.cloned.1.call-done, s32[16384]{0:T(1024)S(1)} %bitcast.36, s32[16384]{0:T(1024)S(1)} %bitcast.35, s32[512]{0:T(512)S(1)} %bitcast.41, s32[512]{0:T(512)S(1)} %bitcast.39, ...), kind=kOutput, calls=%fused_computation.4 | convolution fusion | flops 17230200832 | bytes 34740736 | tf_op jit(solution)/shard_map/dot_general | solution.py:15
  175.2 0.6 broadcast_maximum_fusion
  175.8 4.2 %all-to-all-start.3 = ((f32[4,1,128]{2,1,0:T(1,128)}), f32[4,1,128]{2,1,0:T(1,128)S(1)}, u32[]{:S(2)}, u32[]{:S(2)}) async-start(f32[4,1,128]{2,1,0:T(1,128)} %bitcast.13), calls=%async_computation.3 | async-start | bytes 4096 | tf_op jit(solution)/shard_map/all_to_all | solution.py:61
  180.1 5.1 %all-to-all-done.3 = f32[4,1,128]{2,1,0:T(1,128)S(1)} async-done(((f32[4,1,128]{2,1,0:T(1,128)}), f32[4,1,128]{2,1,0:T(1,128)S(1)}, u32[]{:S(2)}, u32[]{:S(2)}) %all-to-all-start.3) | async-done | bytes 2080 | tf_op jit(solution)/shard_map/all_to_all | solution.py:61
  185.2 2.5 %gather_fusion = f32[256]{0:T(256)} fusion(f32[512]{0:T(512)S(1)} %bitcast.31, s32[1024]{0:T(1024)S(1)} %pad_clamp_fusion), kind=kCustom, calls=%fused_computation | custom fusion | bytes 3072 | tf_op jit(solution)/shard_map/gather | solution.py:64
  (7 shorter events, 0.1 us)
Async XLA Ops:
  6.5 141.6 %all-gather.4.cloned.1.call-start = ((), (), s32[]{:S(2)}) async-start(), calls=%async_computation.4 | async-start | bytes 34603008 | tf_op jit(solution)/shard_map/all_gather | solution.py:51
  35.5 8.4 %all-to-all-start = ((s32[4,1,128]{2,1,0:T(1,128)}), s32[4,1,128]{2,1,0:T(1,128)S(1)}, u32[]{:S(2)}, u32[]{:S(2)}) async-start(s32[4,1,128]{2,1,0:T(1,128)} %bitcast.3), calls=%async_computation | async-start | bytes 4096 | tf_op jit(solution)/shard_map/all_to_all | solution.py:40
  43.9 29.4 %all-to-all-start.1 = ((s32[4,1,128]{2,1,0:T(1,128)}), s32[4,1,128]{2,1,0:T(1,128)S(1)}, u32[]{:S(2)}, u32[]{:S(2)}) async-start(s32[4,1,128]{2,1,0:T(1,128)} %bitcast.7), calls=%async_computation.1 | async-start | bytes 4096 | tf_op jit(solution)/shard_map/all_to_all | solution.py:43
  175.8 9.4 %all-to-all-start.3 = ((f32[4,1,128]{2,1,0:T(1,128)}), f32[4,1,128]{2,1,0:T(1,128)S(1)}, u32[]{:S(2)}, u32[]{:S(2)}) async-start(f32[4,1,128]{2,1,0:T(1,128)} %bitcast.13), calls=%async_computation.3 | async-start | bytes 4096 | tf_op jit(solution)/shard_map/all_to_all | solution.py:61
Sparse Core Ops, SparseCore 0:
  33.5 114.5 all-gather.3
where the time goes:
time: 195 us
  blocking collectives  70.2 us (36%)
  waiting for transfers between devices  58.6 us (30%)
  matrix products  27.1 us (14%)
  between operations  13.4 us (7%)
  starting transfers between devices  10.6 us (5%)
  other arithmetic  7.75 us (4%)
  local copies, waits for them, and re-layouts  6.92 us (4%)
    all_gather x1, waiting for transfers between devices, local(): other_vecs = lax.all_gather(vecs, 'blk', axis=0, tiled=True)  50.3 us
    dot_general x1, matrix products, similarity(): lax.dot_general(left, right, (((1,), (1,)), ((), ())), preferred_element_...  27.1 us
    all_gather x1, blocking collectives, local(): other_keys = lax.all_gather(keys, 'blk', axis=0, tiled=True)  26.2 us
    all_gather x1, blocking collectives, local(): other_order = lax.all_gather(ranks_recv, 'blk', axis=0, tiled=True)  24.5 us
    all_to_all x1, blocking collectives, local(): lax.all_to_all(send_vecs.reshape(groups, capacity, -1), 'corpus', split_a...  19.4 us
    all_to_all x1, waiting for transfers between devices, local(): lax.all_to_all(best.reshape(groups, capacity), 'corpus', split_axis=0, co...  5.12 us
    all_to_all x1, starting transfers between devices, local(): lax.all_to_all(best.reshape(groups, capacity), 'corpus', split_axis=0, co...  4.25 us
  transfers between devices with their start and end apart: 4, of which 3 were waited for; matrix products, arithmetic and copies ran while one was open for 2% of the time, Pallas kernels for 0%

commit v1 on v0

v1 whole, which is shorter than its diff:
```python
import functools

import jax
import jax.numpy as jnp
from jax import lax
from jax.experimental import pallas as pl
from jax.experimental.pallas import tpu as pltpu
from jax.sharding import PartitionSpec as P


AXES = ("corpus", "blk")
ROWS = 256
TAIL = 16
BLOCK = ROWS + TAIL
VMEM_LIMIT = 32 << 20
CLUSTER_STEP = 32768.0


def pair(v):
    return v ^ 1


def cross(v):
    return ((((v - 1) % 4) ^ 1) + 1) % 4


def exchange(name):
    move = {"X": (0, pair), "Z": (1, pair), "Y": (2, pair), "C": (3, pair)}
    move |= {"x": (0, cross), "z": (1, cross), "y": (2, cross)}
    axis, fn = move[name]
    perm = []
    for x in range(4):
        for z in range(4):
            for y in range(4):
                for c in range(2):
                    there = [x, z, y, c]
                    there[axis] = fn(there[axis])
                    a, b, d, e = there
                    perm.append((x * 32 + z * 8 + y * 2 + c, a * 32 + b * 8 + d * 2 + e))
    return perm


PERMS = {name: exchange(name) for name in "XZYCxzy"}


def swap(value, name):
    return lax.ppermute(value, AXES, PERMS[name])


def prepare_kernel(emb_ref, cluster_ref, order_ref, out_ref):
    wide = emb_ref[...].astype(jnp.float32)
    scale = lax.rsqrt(jnp.sum(wide * wide, axis=1, keepdims=True) + 1e-06)
    out_ref[pl.ds(0, ROWS), :] = (wide * scale).astype(jnp.bfloat16)
    order = order_ref[...]
    parts = [cluster_ref[...], order >> 7, order & 127, jnp.zeros_like(order)]
    keys = jnp.concatenate([p.astype(jnp.float32) for p in parts], axis=1)
    out_ref[pl.ds(ROWS, TAIL), :] = jnp.broadcast_to(keys, (TAIL, 4 * ROWS)).astype(jnp.bfloat16)


def prepare(embedding, cluster, order):
    return pl.pallas_call(
        prepare_kernel,
        out_shape=jax.ShapeDtypeStruct((ROWS + TAIL, embedding.shape[1]), jnp.bfloat16),
        in_specs=[pl.BlockSpec(memory_space=pltpu.VMEM)] * 3,
        out_specs=pl.BlockSpec(memory_space=pltpu.VMEM),
    )(embedding, cluster.reshape(1, -1), order.reshape(1, -1))


def pile_keys(pile, i):
    row = pile[pl.ds(i * BLOCK + ROWS, TAIL), :].astype(jnp.float32)[:1]
    return row[:, :ROWS] * CLUSTER_STEP + row[:, ROWS : 2 * ROWS] * 128.0 + row[:, 2 * ROWS : 3 * ROWS]


def nearest_kernel(n_row, n_col, loops, *refs):
    n = len(n_row) + len(n_col)
    rows, cols = refs[: len(n_row)], refs[len(n_row) : n]
    out_ref, best, key_r, base_r, key_c = refs[n:]
    first_row = [sum(n_row[:i]) for i in range(len(n_row))]
    first_col = [sum(n_col[:i]) for i in range(len(n_col))]
    best[...] = jnp.full_like(best, -1.0)
    for p, pile in enumerate(rows):
        for i in range(n_row[p]):
            at = (first_row[p] + i) * BLOCK
            tall = jnp.broadcast_to(pile_keys(pile, i), (128, ROWS)).T
            key_r[pl.ds(at, ROWS), :] = tall
            base_r[pl.ds(at, ROWS), :] = jnp.floor(tall * (1.0 / CLUSTER_STEP)) * CLUSTER_STEP
            key_r[pl.ds(at + ROWS, TAIL), :] = jnp.full((TAIL, 128), -1.0, jnp.float32)
            base_r[pl.ds(at + ROWS, TAIL), :] = jnp.zeros((TAIL, 128), jnp.float32)
    for p, pile in enumerate(cols):
        for i in range(n_col[p]):
            key_c[pl.ds(first_col[p] + i, 1), :] = pile_keys(pile, i)
    for p, c in loops:
        mine = pl.ds(first_row[p] * BLOCK, n_row[p] * BLOCK)

        def tile(j, p=p, c=c, mine=mine):
            start = j * BLOCK if isinstance(j, int) else pl.multiple_of(j * BLOCK, TAIL)
            sims = lax.dot_general(
                rows[p][...],
                cols[c][pl.ds(start, ROWS), :],
                (((1,), (1,)), ((), ())),
                preferred_element_type=jnp.float32,
            )
            theirs = key_c[pl.ds(first_col[c] + j, 1), :]
            top = best[mine, :]
            for q in range(ROWS // 128):
                lanes = slice(q * 128, (q + 1) * 128)
                keep = (theirs[:, lanes] < key_r[mine, :]) & (theirs[:, lanes] >= base_r[mine, :])
                top = jnp.maximum(top, jnp.where(keep, sims[:, lanes], -1.0))
            best[mine, :] = top

        if n_row[p] == 1:
            for j in range(n_col[c]):
                tile(j)
        else:
            lax.fori_loop(0, n_col[c], lambda j, carry, tile=tile: (tile(j), carry)[1], 0)
    for b in range(sum(n_row)):
        out_ref[pl.ds(b, 1), :] = jnp.max(best[pl.ds(b * BLOCK, ROWS), :].T, axis=0, keepdims=True)


def nearest(rows, cols, loops=None):
    n_row = tuple(v.shape[0] // BLOCK for v in rows)
    n_col = tuple(v.shape[0] // BLOCK for v in cols)
    loops = loops or tuple((r, c) for r in range(len(rows)) for c in range(len(cols)))
    width = rows[0].shape[1]
    tall = sum(n_row) * BLOCK
    return pl.pallas_call(
        functools.partial(nearest_kernel, n_row, n_col, loops),
        out_shape=jax.ShapeDtypeStruct((sum(n_row), ROWS), jnp.float32),
        in_specs=[pl.BlockSpec(memory_space=pltpu.VMEM)] * (len(rows) + len(cols)),
        out_specs=pl.BlockSpec(memory_space=pltpu.VMEM),
        scratch_shapes=[
            pltpu.VMEM((tall, 128), jnp.float32),
            pltpu.VMEM((tall, 128), jnp.float32),
            pltpu.VMEM((tall, 128), jnp.float32),
            pltpu.VMEM((sum(n_col), ROWS), jnp.float32),
        ],
        compiler_params=pltpu.CompilerParams(vmem_limit_bytes=VMEM_LIMIT),
        cost_estimate=pl.CostEstimate(
            flops=2 * sum(n_row[r] * n_col[c] for r, c in loops) * ROWS * ROWS * width,
            bytes_accessed=(sum(n_row) + sum(n_col)) * ROWS * width * 2,
            transcendentals=0,
        ),
    )(*rows, *cols)


def near(own, names):
    return {"": own} | {k: swap(own, k) for k in names}


def mid(got, names):
    pairs = [(names[i], names[(i + 1) % 3]) for i in range(3)]
    return [swap(got[k], link) for link, k in pairs]


def stacked(*blocks):
    return jnp.concatenate(blocks, axis=0)


def steps(embedding, cluster, order):
    own = prepare(embedding, cluster, order)
    b_names, a_names = "xzy", "XZY"
    b = near(own, b_names)
    a = near(own, a_names)
    b_mid = mid(b, b_names)
    a_mid = mid(a, a_names)
    near_a = stacked(*(a[k] for k in ("", *a_names)))
    other = swap(stacked(*(b[k] for k in b_names)), "C")
    near_b = stacked(*(b[k] for k in ("", *b_names)), swap(own, "C"))
    r1 = nearest([near_a], [near_b])
    b_mid, r1 = lax.optimization_barrier((b_mid, r1))
    b_far = swap(b_mid[1], "x")
    mid_b = stacked(*b_mid)
    mid_other = swap(mid_b, "C")
    r2 = nearest([near_a], [other, mid_b])
    a_mid, mid_other, r2 = lax.optimization_barrier((a_mid, mid_other, r2))
    a_far = swap(a_mid[1], "X")
    mid_a = stacked(*a_mid)
    both_a = stacked(near_a, mid_a)
    r3a = nearest([both_a], [mid_other])
    r3b = nearest([mid_a], [near_b, other, mid_b])
    b_far, a_far, r3a, r3b = lax.optimization_barrier((b_far, a_far, r3a, r3b))
    far_b = stacked(b_far, swap(b_far, "C"))
    r4a = nearest([a_far], [near_b, other, mid_b, mid_other])
    r4b = nearest([stacked(both_a, a_far)], [far_b])
    r3 = jnp.concatenate([jnp.maximum(jnp.maximum(r1, r2), r3a[:4]), jnp.maximum(r3b, r3a[4:]), r4a], axis=0)
    best = jnp.maximum(r3, r4b)
    names = ["", *a_names, "XZ", "ZY", "XY", "XZY"]
    slot = {k: best[i : i + 1] for i, k in enumerate(names)}
    x = swap(jnp.concatenate([slot[k] for k in ("X", "XZ", "XY", "XZY")], axis=0), "X")
    kept = jnp.maximum(x, jnp.concatenate([slot[k] for k in ("", "Z", "Y", "ZY")], axis=0))
    z = swap(jnp.concatenate([kept[1:2], kept[3:4]], axis=0), "Z")
    kept = jnp.maximum(z, jnp.concatenate([kept[0:1], kept[2:3]], axis=0))
    return jnp.maximum(swap(kept[1], "Y"), kept[0])


def solution(mesh):
    in_specs = (P(AXES, None), P(AXES), P(AXES))
    return jax.shard_map(steps, mesh=mesh, in_specs=in_specs, out_specs=P(AXES), check_vma=False)
```

time: 195 us -> 96.3 us (0.49)
  blocking collectives: 70.2 us -> 0 us
  Pallas kernels: 0 us -> 30.5 us
  matrix products: 27.1 us -> 0 us
  waiting for transfers between devices: 58.6 us -> 36.2 us
  starting transfers between devices: 10.6 us -> 25.4 us
  between operations: 13.4 us -> 0.31 us
  other arithmetic: 7.75 us -> 1.15 us
  local copies, waits for them, and re-layouts: 6.92 us -> 2.52 us
    all_gather x2 -> x0, blocking collectives: 50.8 us -> none  [the longest x1 26.2 us: local(): other_keys = lax.all_gather(keys, 'blk', axis=0, tiled=True)]
    all_gather x1 -> x0, waiting for transfers between devices: 50.3 us -> none  [local(): other_vecs = lax.all_gather(vecs, 'blk', axis=0, tiled=True)]
    ppermute x0 -> x21, waiting for transfers between devices: none -> 36.2 us  [swap(): return lax.ppermute(value, AXES, PERMS[name])]
    pallas_call x0 -> x7, Pallas kernels: none -> 30.5 us  [the longest x6 28.5 us: nearest(): pl.pallas_call(functools.partial(nearest_kernel, n_row, n_col, loops), ou...]
    dot_general x1 -> x0, matrix products: 27.1 us -> none  [similarity(): lax.dot_general(left, right, (((1,), (1,)), ((), ())), preferred_element_...]
    ppermute x0 -> x21, starting transfers between devices: none -> 25.4 us  [swap(): return lax.ppermute(value, AXES, PERMS[name])]
    all_to_all x1 -> x0, blocking collectives: 19.4 us -> none  [local(): lax.all_to_all(send_vecs.reshape(groups, capacity, -1), 'corpus', split_a...]
    all_to_all x3 -> x0, starting transfers between devices: 10.6 us -> none  [the longest x1 4.25 us: local(): lax.all_to_all(best.reshape(groups, capacity), 'corpus', split_axis=0, co...]
  transfers between devices with their start and end apart: 4 -> 21, of which waited for: 3 -> 14; matrix products, arithmetic and copies ran while one was open for 2% -> 3% of each run, Pallas kernels for 0% -> 26%
where the time goes in v1:
time: 96.3 us; the launch traced here: 96.1 us
  waiting for transfers between devices  36.2 us (38%)
  Pallas kernels  30.5 us (32%)
  starting transfers between devices  25.4 us (26%)
  local copies, waits for them, and re-layouts  2.52 us (3%)
  other arithmetic  1.15 us (1%)
    ppermute x21, waiting for transfers between devices, swap(): return lax.ppermute(value, AXES, PERMS[name])  36.2 us
    pallas_call x6, Pallas kernels, nearest(): pl.pallas_call(functools.partial(nearest_kernel, n_row, n_col, loops), ou...  28.5 us
    ppermute x21, starting transfers between devices, swap(): return lax.ppermute(value, AXES, PERMS[name])  25.4 us
    unnamed x13, local copies, waits for them, and re-layouts  2.22 us
    pallas_call x1, Pallas kernels, prepare(): pl.pallas_call(prepare_kernel, out_shape=jax.ShapeDtypeStruct((ROWS + TAI...  2.06 us
  transfers between devices with their start and end apart: 21, of which 14 were waited for; matrix products, arithmetic and copies ran while one was open for 3% of the time, Pallas kernels for 26%

profile of v1, /device:TPU:0, one launch (start us, length us, event | category | flops | bytes accessed | tf_op | source)
XLA Modules:
  0.0 96.1 jit_solution(8982352138388272451)
XLA Ops:
  0.0 2.1 %shard_map.37 = bf16[272,1024]{1,0:T(8,128)(2,1)} custom-call(bf16[256,1024]{1,0:T(8,128)(2,1)} %emb_ref.1, s32[1,256]{1,0:T(1,128)} %bitcast.6, s32[1,256]{1,0:T(1,128)} %bitcast.7), custom_call_target="tpu_custom_call" | custom-call | tf_op jit(solution)/shard_map/pallas_call | solution.py:61
  2.1 4.1 %collective-permute-start = (bf16[272,1024]{1,0:T(8,128)(2,1)}, bf16[272,1024]{1,0:T(8,128)(2,1)S(1)}, u32[]{:S(2)}, u32[]{:S(2)}) collective-permute-start(bf16[272,1024]{1,0:T(8,128)(2,1)} %shard_map.37), channel_id=1, source_target_pairs={{0,24},{1,25},{2,26},{3,27},{4,28},{5,29},{6,30},{7,31},{8,16},{9,... | collective-permute-start | bytes 1671176 | tf_op jit(solution)/shard_map/ppermute | solution.py:47
  6.2 3.0 %collective-permute-start.2 = (bf16[272,1024]{1,0:T(8,128)(2,1)}, bf16[272,1024]{1,0:T(8,128)(2,1)S(1)}, u32[]{:S(2)}, u32[]{:S(2)}) collective-permute-start(bf16[272,1024]{1,0:T(8,128)(2,1)} %shard_map.37), channel_id=1, source_target_pairs={{0,6},{1,7},{2,4},{3,5},{4,2},{5,3},{6,0},{7,1},{8,14},{9,15},{10,... | collective-permute-start | bytes 1671176 | tf_op jit(solution)/shard_map/ppermute | solution.py:47
  9.2 2.8 %collective-permute-start.4 = (bf16[272,1024]{1,0:T(8,128)(2,1)}, bf16[272,1024]{1,0:T(8,128)(2,1)S(1)}, u32[]{:S(2)}, u32[]{:S(2)}) collective-permute-start(bf16[272,1024]{1,0:T(8,128)(2,1)} %shard_map.37), channel_id=1, source_target_pairs={{0,96},{1,97},{2,98},{3,99},{4,100},{5,101},{6,102},{7,103},{8,104... | collective-permute-start | bytes 1671176 | tf_op jit(solution)/shard_map/ppermute | solution.py:47
  12.0 0.2 collective-permute-start.6
  12.2 1.3 %constant_dynamic-update-slice_fusion.14 = (bf16[1904,1024]{1,0:T(8,128)(2,1)S(1)}, bf16[2176,1024]{1,0:T(8,128)(2,1)S(1)}, bf16[1360,1024]{1,0:T(8,128)(2,1)S(1)}) fusion(bf16[272,1024]{1,0:T(8,128)(2,1)} %shard_map.37), kind=kLoop, calls=%fused_computation.18 | loop fusion | bytes 2228224
  13.5 5.5 %collective-permute-done = bf16[272,1024]{1,0:T(8,128)(2,1)S(1)} collective-permute-done((bf16[272,1024]{1,0:T(8,128)(2,1)}, bf16[272,1024]{1,0:T(8,128)(2,1)S(1)}, u32[]{:S(2)}, u32[]{:S(2)}) %collective-permute-start) | collective-permute-done | bytes 557088 | tf_op jit(solution)/shard_map/ppermute | solution.py:47
  19.0 2.8 %collective-permute-done.2 = bf16[272,1024]{1,0:T(8,128)(2,1)S(1)} collective-permute-done((bf16[272,1024]{1,0:T(8,128)(2,1)}, bf16[272,1024]{1,0:T(8,128)(2,1)S(1)}, u32[]{:S(2)}, u32[]{:S(2)}) %collective-permute-start.2) | collective-permute-done | bytes 557088 | tf_op jit(solution)/shard_map/ppermute | solution.py:47
  21.8 0.3 collective-permute-start.8
  22.1 2.4 %collective-permute-done.4 = bf16[272,1024]{1,0:T(8,128)(2,1)S(1)} collective-permute-done((bf16[272,1024]{1,0:T(8,128)(2,1)}, bf16[272,1024]{1,0:T(8,128)(2,1)S(1)}, u32[]{:S(2)}, u32[]{:S(2)}) %collective-permute-start.4) | collective-permute-done | bytes 557088 | tf_op jit(solution)/shard_map/ppermute | solution.py:47
  24.4 0.1 pad_maximum_fusion.1
  24.8 2.8 %collective-permute-start.1 = (bf16[272,1024]{1,0:T(8,128)(2,1)S(1)}, bf16[272,1024]{1,0:T(8,128)(2,1)S(1)}, u32[]{:S(2)}, u32[]{:S(2)}) collective-permute-start(bf16[272,1024]{1,0:T(8,128)(2,1)S(1)} %collective-permute-done), channel_id=1, source_target_pairs={{0,96},{1,97},{2,98},{3,99},{4,100},{5,101},{6,102},{7,103},{8,104... | collective-permute-start | bytes 1671176 | tf_op jit(solution)/shard_map/ppermute | solution.py:47
  27.7 0.4 collective-permute-start.3
  28.1 5.0 %collective-permute-done.7 = bf16[272,1024]{1,0:T(8,128)(2,1)S(1)} collective-permute-done((bf16[272,1024]{1,0:T(8,128)(2,1)}, bf16[272,1024]{1,0:T(8,128)(2,1)S(1)}, u32[]{:S(2)}, u32[]{:S(2)}) %collective-permute-start.7) | collective-permute-done | bytes 557088 | tf_op jit(solution)/shard_map/ppermute | solution.py:47
  33.0 3.0 %collective-permute-start.5 = (bf16[272,1024]{1,0:T(8,128)(2,1)S(1)}, bf16[272,1024]{1,0:T(8,128)(2,1)S(1)}, u32[]{:S(2)}, u32[]{:S(2)}) collective-permute-start(bf16[272,1024]{1,0:T(8,128)(2,1)S(1)} %collective-permute-done.4), channel_id=1, source_target_pairs={{0,6},{1,7},{2,4},{3,5},{4,2},{5,3},{6,0},{7,1},{8,14},{9,15},{10,... | collective-permute-start | bytes 1671176 | tf_op jit(solution)/shard_map/ppermute | solution.py:47
  36.1 0.2 pad_maximum_fusion.refs_0_
  36.3 4.5 %shard_map.38 = f32[4,256]{1,0:T(4,128)S(1)} custom-call(bf16[1088,1024]{1,0:T(8,128)(2,1)S(1)} %pad_maximum_fusion.refs_0_, bf16[1360,1024]{1,0:T(8,128)(2,1)S(1)} %constant_dynamic-update-slice_fusion.refs_1_), custom_call_target="tpu_custom_call" | custom-call | flops 2684354560 | bytes 4718592 | tf_op jit(solution)/shard_map/pallas_call | solution.py:126
  40.7 0.4 collective-permute-done.1
  41.1 2.6 %collective-permute-done.3 = bf16[272,1024]{1,0:T(8,128)(2,1)S(1)} collective-permute-done((bf16[272,1024]{1,0:T(8,128)(2,1)S(1)}, bf16[272,1024]{1,0:T(8,128)(2,1)S(1)}, u32[]{:S(2)}, u32[]{:S(2)}) %collective-permute-start.3) | collective-permute-done | bytes 557088 | tf_op jit(solution)/shard_map/ppermute | solution.py:47
  43.7 3.5 %collective-permute-done.5 = bf16[272,1024]{1,0:T(8,128)(2,1)S(1)} collective-permute-done((bf16[272,1024]{1,0:T(8,128)(2,1)S(1)}, bf16[272,1024]{1,0:T(8,128)(2,1)S(1)}, u32[]{:S(2)}, u32[]{:S(2)}) %collective-permute-start.5) | collective-permute-done | bytes 557088 | tf_op jit(solution)/shard_map/ppermute | solution.py:47
  47.5 1.6 %collective-permute-start.10 = (bf16[272,1024]{1,0:T(8,128)(2,1)S(1)}, bf16[272,1024]{1,0:T(8,128)(2,1)S(1)}, u32[]{:S(2)}, u32[]{:S(2)}) collective-permute-start(bf16[272,1024]{1,0:T(8,128)(2,1)S(1)} %collective-permute-done.7), channel_id=1, source_target_pairs={{0,32},{1,33},{2,34},{3,35},{4,36},{5,37},{6,38},{7,39},{8,40},{9,... | collective-permute-start | bytes 1671176 | tf_op jit(solution)/shard_map/ppermute | solution.py:47
  49.0 0.6 collective-permute-start.11
  49.6 0.3 collective-permute-start.12
  49.9 0.1 constant_dynamic-update-slice_fusion.13
  50.1 0.2 constant_dynamic-update-slice_fusion.12
  50.2 0.2 constant_dynamic-update-slice_fusion.11
  50.4 2.2 %collective-permute-start.15 = (bf16[272,1024]{1,0:T(8,128)(2,1)S(1)}, bf16[272,1024]{1,0:T(8,128)(2,1)S(1)}, u32[]{:S(2)}, u32[]{:S(2)}) collective-permute-start(bf16[272,1024]{1,0:T(8,128)(2,1)S(1)} %collective-permute-done.3), channel_id=1, source_target_pairs={{0,96},{1,97},{2,98},{3,99},{4,100},{5,101},{6,102},{7,103},{8,104... | collective-permute-start | bytes 1671176 | tf_op jit(solution)/shard_map/ppermute | solution.py:47
  52.6 5.3 %shard_map.39 = f32[4,256]{1,0:T(4,128)S(1)} custom-call(bf16[1088,1024]{1,0:T(8,128)(2,1)S(1)} %pad_maximum_fusion.refs_0_, bf16[816,1024]{1,0:T(8,128)(2,1)S(1)} %collective-permute-done.14.refs_1_.refs_2_, bf16[816,1024]{1,0:T(8,128)(2,1)S(1)} %constant_dynamic-update-slice_fusion.5.refs_2_.refs_3_), custom_call_target="tpu_custom_call" | custom-call | flops 3221225472 | bytes 5242880 | tf_op jit(solution)/shard_map/pallas_call | solution.py:126
  57.9 4.6 %collective-permute-done.10 = bf16[272,1024]{1,0:T(8,128)(2,1)S(1)} collective-permute-done((bf16[272,1024]{1,0:T(8,128)(2,1)S(1)}, bf16[272,1024]{1,0:T(8,128)(2,1)S(1)}, u32[]{:S(2)}, u32[]{:S(2)}) %collective-permute-start.10) | collective-permute-done | bytes 557088 | tf_op jit(solution)/shard_map/ppermute | solution.py:47
  62.5 1.2 %collective-permute-done.11 = bf16[272,1024]{1,0:T(8,128)(2,1)S(1)} collective-permute-done((bf16[272,1024]{1,0:T(8,128)(2,1)S(1)}, bf16[272,1024]{1,0:T(8,128)(2,1)S(1)}, u32[]{:S(2)}, u32[]{:S(2)}) %collective-permute-start.11) | collective-permute-done | bytes 557088 | tf_op jit(solution)/shard_map/ppermute | solution.py:47
  63.7 0.3 collective-permute-done.12
  64.0 0.5 collective-permute-start.16
  64.5 0.1 constant_dynamic-update-slice_fusion.10
  64.7 0.2 constant_dynamic-update-slice_fusion.9
  64.9 0.2 constant_dynamic-update-slice_fusion.8
  65.0 4.6 %shard_map.40 = f32[7,256]{1,0:T(8,128)S(1)} custom-call(bf16[1904,1024]{1,0:T(8,128)(2,1)S(1)} %get-tuple-element.31.refs_0_, bf16[816,1024]{1,0:T(8,128)(2,1)S(1)} %collective-permute-done.13.refs_1_.refs_4_), custom_call_target="tpu_custom_call" | custom-call | flops 2818572288 | bytes 5242880 | tf_op jit(solution)/shard_map/pallas_call | solution.py:126
  69.6 0.1 pad_maximum_fusion.2.refs_0_
  69.8 7.4 %shard_map.41 = f32[3,256]{1,0:T(4,128)S(1)} custom-call(bf16[816,1024]{1,0:T(8,128)(2,1)S(1)} %pad_maximum_fusion.2.refs_0_, bf16[1360,1024]{1,0:T(8,128)(2,1)S(1)} %constant_dynamic-update-slice_fusion.refs_1_, bf16[816,1024]{1,0:T(8,128)(2,1)S(1)} %collective-permute-done.14.refs_1_.refs_2_, ...), custom_call_target="tpu_custom_call" | custom-call | flops 4429185024 | bytes 7340032 | tf_op jit(solution)/shard_map/pallas_call | solution.py:126
  77.2 0.4 collective-permute-done.16.refs_0_
  77.5 3.0 %shard_map.42 = f32[1,256]{1,0:T(1,128)S(1)} custom-call(bf16[272,1024]{1,0:T(8,128)(2,1)S(1)} %collective-permute-done.16.refs_0_, bf16[1360,1024]{1,0:T(8,128)(2,1)S(1)} %constant_dynamic-update-slice_fusion.refs_1_, bf16[816,1024]{1,0:T(8,128)(2,1)S(1)} %collective-permute-done.14.refs_1_.refs_2_, ...), custom_call_target="tpu_custom_call" | custom-call | flops 1879048192 | bytes 7864320 | tf_op jit(solution)/shard_map/pallas_call | solution.py:126
  80.7 3.7 %shard_map.43 = f32[8,256]{1,0:T(8,128)S(1)} custom-call(bf16[2176,1024]{1,0:T(8,128)(2,1)S(1)} %constant_dynamic-update-slice_fusion.15.refs_0_, bf16[544,1024]{1,0:T(8,128)(2,1)S(1)} %pad_maximum_fusion.3.refs_1_), custom_call_target="tpu_custom_call" | custom-call | flops 2147483648 | bytes 5242880 | tf_op jit(solution)/shard_map/pallas_call | solution.py:126
  84.5 1.5 %collective-permute-start.18 = (f32[4,256]{1,0:T(4,128)S(1)}, f32[4,256]{1,0:T(4,128)S(1)}, u32[]{:S(2)}, u32[]{:S(2)}) collective-permute-start(f32[4,256]{1,0:T(4,128)S(1)} %pad_maximum_fusion.4), channel_id=1, source_target_pairs={{0,32},{1,33},{2,34},{3,35},{4,36},{5,37},{6,38},{7,39},{8,40},{9,... | collective-permute-start | bytes 12296 | tf_op jit(solution)/shard_map/ppermute | solution.py:47
  86.0 2.2 %collective-permute-done.18 = f32[4,256]{1,0:T(4,128)S(1)} collective-permute-done((f32[4,256]{1,0:T(4,128)S(1)}, f32[4,256]{1,0:T(4,128)S(1)}, u32[]{:S(2)}, u32[]{:S(2)}) %collective-permute-start.18) | collective-permute-done | bytes 4128 | tf_op jit(solution)/shard_map/ppermute | solution.py:47
  88.2 1.6 %collective-permute-start.19 = (f32[2,256]{1,0:T(2,128)S(1)}, f32[2,256]{1,0:T(2,128)S(1)}, u32[]{:S(2)}, u32[]{:S(2)}) collective-permute-start(f32[2,256]{1,0:T(2,128)S(1)} %pad_maximum_fusion.5), channel_id=1, source_target_pairs={{0,8},{1,9},{2,10},{3,11},{4,12},{5,13},{6,14},{7,15},{8,0},{9,1},... | collective-permute-start | bytes 6152 | tf_op jit(solution)/shard_map/ppermute | solution.py:47
  89.8 2.1 %collective-permute-done.19 = f32[2,256]{1,0:T(2,128)S(1)} collective-permute-done((f32[2,256]{1,0:T(2,128)S(1)}, f32[2,256]{1,0:T(2,128)S(1)}, u32[]{:S(2)}, u32[]{:S(2)}) %collective-permute-start.19) | collective-permute-done | bytes 2080 | tf_op jit(solution)/shard_map/ppermute | solution.py:47
  91.9 0.4 collective-permute-start.20
  92.3 3.3 %collective-permute-done.20 = f32[256]{0:T(256)S(1)} collective-permute-done((f32[256]{0:T(256)S(1)}, f32[256]{0:T(256)S(1)}, u32[]{:S(2)}, u32[]{:S(2)}) %collective-permute-start.20) | collective-permute-done | bytes 1056 | tf_op jit(solution)/shard_map/ppermute | solution.py:47
  95.6 0.6 max.27
  (34 shorter events, 0.7 us)
Async XLA Ops:
  2.1 17.0 %collective-permute-start = (bf16[272,1024]{1,0:T(8,128)(2,1)}, bf16[272,1024]{1,0:T(8,128)(2,1)S(1)}, u32[]{:S(2)}, u32[]{:S(2)}) collective-permute-start(bf16[272,1024]{1,0:T(8,128)(2,1)} %shard_map.37), channel_id=1, source_target_pairs={{0,24},{1,25},{2,26},{3,27},{4,28},{5,29},{6,30},{7,31},{8,16},{9,... | collective-permute-start | bytes 1671176 | tf_op jit(solution)/shard_map/ppermute | solution.py:47
  6.2 15.6 %collective-permute-start.2 = (bf16[272,1024]{1,0:T(8,128)(2,1)}, bf16[272,1024]{1,0:T(8,128)(2,1)S(1)}, u32[]{:S(2)}, u32[]{:S(2)}) collective-permute-start(bf16[272,1024]{1,0:T(8,128)(2,1)} %shard_map.37), channel_id=1, source_target_pairs={{0,6},{1,7},{2,4},{3,5},{4,2},{5,3},{6,0},{7,1},{8,14},{9,15},{10,... | collective-permute-start | bytes 1671176 | tf_op jit(solution)/shard_map/ppermute | solution.py:47
  9.2 15.2 %collective-permute-start.4 = (bf16[272,1024]{1,0:T(8,128)(2,1)}, bf16[272,1024]{1,0:T(8,128)(2,1)S(1)}, u32[]{:S(2)}, u32[]{:S(2)}) collective-permute-start(bf16[272,1024]{1,0:T(8,128)(2,1)} %shard_map.37), channel_id=1, source_target_pairs={{0,96},{1,97},{2,98},{3,99},{4,100},{5,101},{6,102},{7,103},{8,104... | collective-permute-start | bytes 1671176 | tf_op jit(solution)/shard_map/ppermute | solution.py:47
  12.0 15.7 %collective-permute-start.6 = (bf16[272,1024]{1,0:T(8,128)(2,1)}, bf16[272,1024]{1,0:T(8,128)(2,1)S(1)}, u32[]{:S(2)}, u32[]{:S(2)}) collective-permute-start(bf16[272,1024]{1,0:T(8,128)(2,1)} %shard_map.37), channel_id=1, source_target_pairs={{0,32},{1,33},{2,34},{3,35},{4,36},{5,37},{6,38},{7,39},{8,40},{9,... | collective-permute-start | bytes 1671176 | tf_op jit(solution)/shard_map/ppermute | solution.py:47
  12.2 12.6 %collective-permute-start.9 = (bf16[272,1024]{1,0:T(8,128)(2,1)}, bf16[272,1024]{1,0:T(8,128)(2,1)S(1)}, u32[]{:S(2)}, u32[]{:S(2)}) collective-permute-start(bf16[272,1024]{1,0:T(8,128)(2,1)} %shard_map.37), channel_id=1, source_target_pairs={{0,1},{1,0},{2,3},{3,2},{4,5},{5,4},{6,7},{7,6},{8,9},{9,8},{10,11... | collective-permute-start | bytes 1671176 | tf_op jit(solution)/shard_map/ppermute | solution.py:47
  13.5 22.6 %copy-start = (bf16[272,1024]{1,0:T(8,128)(2,1)S(1)}, bf16[272,1024]{1,0:T(8,128)(2,1)}, u32[]{:S(2)}) copy-start(bf16[272,1024]{1,0:T(8,128)(2,1)} %shard_map.37) | copy-start | bytes 1671172
  19.0 14.0 %collective-permute-start.7 = (bf16[272,1024]{1,0:T(8,128)(2,1)}, bf16[272,1024]{1,0:T(8,128)(2,1)S(1)}, u32[]{:S(2)}, u32[]{:S(2)}) collective-permute-start(bf16[272,1024]{1,0:T(8,128)(2,1)} %shard_map.37), channel_id=1, source_target_pairs={{0,8},{1,9},{2,10},{3,11},{4,12},{5,13},{6,14},{7,15},{8,0},{9,1},... | collective-permute-start | bytes 1671176 | tf_op jit(solution)/shard_map/ppermute | solution.py:47
  21.8 14.3 %collective-permute-start.8 = (bf16[272,1024]{1,0:T(8,128)(2,1)}, bf16[272,1024]{1,0:T(8,128)(2,1)S(1)}, u32[]{:S(2)}, u32[]{:S(2)}) collective-permute-start(bf16[272,1024]{1,0:T(8,128)(2,1)} %shard_map.37), channel_id=1, source_target_pairs={{0,2},{1,3},{2,0},{3,1},{4,6},{5,7},{6,4},{7,5},{8,10},{9,11},{10,... | collective-permute-start | bytes 1671176 | tf_op jit(solution)/shard_map/ppermute | solution.py:47
  24.6 25.8 %collective-permute-start.14 = (bf16[816,1024]{1,0:T(8,128)(2,1)S(1)}, bf16[816,1024]{1,0:T(8,128)(2,1)S(1)}, u32[]{:S(2)}, u32[]{:S(2)}) collective-permute-start(bf16[816,1024]{1,0:T(8,128)(2,1)S(1)} %pad_maximum_fusion.1), channel_id=1, source_target_pairs={{0,1},{1,0},{2,3},{3,2},{4,5},{5,4},{6,7},{7,6},{8,9},{9,8},{10,11... | collective-permute-start | bytes 5013512 | tf_op jit(solution)/shard_map/ppermute | solution.py:47
  24.8 16.3 %collective-permute-start.1 = (bf16[272,1024]{1,0:T(8,128)(2,1)S(1)}, bf16[272,1024]{1,0:T(8,128)(2,1)S(1)}, u32[]{:S(2)}, u32[]{:S(2)}) collective-permute-start(bf16[272,1024]{1,0:T(8,128)(2,1)S(1)} %collective-permute-done), channel_id=1, source_target_pairs={{0,96},{1,97},{2,98},{3,99},{4,100},{5,101},{6,102},{7,103},{8,104... | collective-permute-start | bytes 1671176 | tf_op jit(solution)/shard_map/ppermute | solution.py:47
  27.7 16.0 %collective-permute-start.3 = (bf16[272,1024]{1,0:T(8,128)(2,1)S(1)}, bf16[272,1024]{1,0:T(8,128)(2,1)S(1)}, u32[]{:S(2)}, u32[]{:S(2)}) collective-permute-start(bf16[272,1024]{1,0:T(8,128)(2,1)S(1)} %collective-permute-done.2), channel_id=1, source_target_pairs={{0,24},{1,25},{2,26},{3,27},{4,28},{5,29},{6,30},{7,31},{8,16},{9,... | collective-permute-start | bytes 1671176 | tf_op jit(solution)/shard_map/ppermute | solution.py:47
  33.0 14.2 %collective-permute-start.5 = (bf16[272,1024]{1,0:T(8,128)(2,1)S(1)}, bf16[272,1024]{1,0:T(8,128)(2,1)S(1)}, u32[]{:S(2)}, u32[]{:S(2)}) collective-permute-start(bf16[272,1024]{1,0:T(8,128)(2,1)S(1)} %collective-permute-done.4), channel_id=1, source_target_pairs={{0,6},{1,7},{2,4},{3,5},{4,2},{5,3},{6,0},{7,1},{8,14},{9,15},{10,... | collective-permute-start | bytes 1671176 | tf_op jit(solution)/shard_map/ppermute | solution.py:47
  47.4 16.6 %collective-permute-start.13 = (bf16[816,1024]{1,0:T(8,128)(2,1)S(1)}, bf16[816,1024]{1,0:T(8,128)(2,1)S(1)}, u32[]{:S(2)}, u32[]{:S(2)}) collective-permute-start(bf16[816,1024]{1,0:T(8,128)(2,1)S(1)} %constant_dynamic-update-slice_fusion.5.refs_2_.refs_3_), channel_id=1, source_target_pairs={{0,1},{1,0},{2,3},{3,2},{4,5},{5,4},{6,7},{7,6},{8,9},{9,8},{10,11... | collective-permute-start | bytes 5013512 | tf_op jit(solution)/shard_map/ppermute | solution.py:47
  47.5 15.0 %collective-permute-start.10 = (bf16[272,1024]{1,0:T(8,128)(2,1)S(1)}, bf16[272,1024]{1,0:T(8,128)(2,1)S(1)}, u32[]{:S(2)}, u32[]{:S(2)}) collective-permute-start(bf16[272,1024]{1,0:T(8,128)(2,1)S(1)} %collective-permute-done.7), channel_id=1, source_target_pairs={{0,32},{1,33},{2,34},{3,35},{4,36},{5,37},{6,38},{7,39},{8,40},{9,... | collective-permute-start | bytes 1671176 | tf_op jit(solution)/shard_map/ppermute | solution.py:47
  49.0 14.7 %collective-permute-start.11 = (bf16[272,1024]{1,0:T(8,128)(2,1)S(1)}, bf16[272,1024]{1,0:T(8,128)(2,1)S(1)}, u32[]{:S(2)}, u32[]{:S(2)}) collective-permute-start(bf16[272,1024]{1,0:T(8,128)(2,1)S(1)} %collective-permute-done.8), channel_id=1, source_target_pairs={{0,8},{1,9},{2,10},{3,11},{4,12},{5,13},{6,14},{7,15},{8,0},{9,1},... | collective-permute-start | bytes 1671176 | tf_op jit(solution)/shard_map/ppermute | solution.py:47
  49.6 14.4 %collective-permute-start.12 = (bf16[272,1024]{1,0:T(8,128)(2,1)S(1)}, bf16[272,1024]{1,0:T(8,128)(2,1)S(1)}, u32[]{:S(2)}, u32[]{:S(2)}) collective-permute-start(bf16[272,1024]{1,0:T(8,128)(2,1)S(1)} %collective-permute-done.6), channel_id=1, source_target_pairs={{0,2},{1,3},{2,0},{3,1},{4,6},{5,7},{6,4},{7,5},{8,10},{9,11},{10,... | collective-permute-start | bytes 1671176 | tf_op jit(solution)/shard_map/ppermute | solution.py:47
  50.4 26.8 %collective-permute-start.15 = (bf16[272,1024]{1,0:T(8,128)(2,1)S(1)}, bf16[272,1024]{1,0:T(8,128)(2,1)S(1)}, u32[]{:S(2)}, u32[]{:S(2)}) collective-permute-start(bf16[272,1024]{1,0:T(8,128)(2,1)S(1)} %collective-permute-done.3), channel_id=1, source_target_pairs={{0,96},{1,97},{2,98},{3,99},{4,100},{5,101},{6,102},{7,103},{8,104... | collective-permute-start | bytes 1671176 | tf_op jit(solution)/shard_map/ppermute | solution.py:47
  64.0 13.5 %collective-permute-start.16 = (bf16[272,1024]{1,0:T(8,128)(2,1)S(1)}, bf16[272,1024]{1,0:T(8,128)(2,1)S(1)}, u32[]{:S(2)}, u32[]{:S(2)}) collective-permute-start(bf16[272,1024]{1,0:T(8,128)(2,1)S(1)} %collective-permute-done.11), channel_id=1, source_target_pairs={{0,32},{1,33},{2,34},{3,35},{4,36},{5,37},{6,38},{7,39},{8,40},{9,... | collective-permute-start | bytes 1671176 | tf_op jit(solution)/shard_map/ppermute | solution.py:47
  77.5 3.1 %collective-permute-start.17 = (bf16[272,1024]{1,0:T(8,128)(2,1)S(1)}, bf16[272,1024]{1,0:T(8,128)(2,1)S(1)}, u32[]{:S(2)}, u32[]{:S(2)}) collective-permute-start(bf16[272,1024]{1,0:T(8,128)(2,1)S(1)} %collective-permute-done.15), channel_id=1, source_target_pairs={{0,1},{1,0},{2,3},{3,2},{4,5},{5,4},{6,7},{7,6},{8,9},{9,8},{10,11... | collective-permute-start | bytes 1671176 | tf_op jit(solution)/shard_map/ppermute | solution.py:47
  84.5 3.7 %collective-permute-start.18 = (f32[4,256]{1,0:T(4,128)S(1)}, f32[4,256]{1,0:T(4,128)S(1)}, u32[]{:S(2)}, u32[]{:S(2)}) collective-permute-start(f32[4,256]{1,0:T(4,128)S(1)} %pad_maximum_fusion.4), channel_id=1, source_target_pairs={{0,32},{1,33},{2,34},{3,35},{4,36},{5,37},{6,38},{7,39},{8,40},{9,... | collective-permute-start | bytes 12296 | tf_op jit(solution)/shard_map/ppermute | solution.py:47
  88.2 3.7 %collective-permute-start.19 = (f32[2,256]{1,0:T(2,128)S(1)}, f32[2,256]{1,0:T(2,128)S(1)}, u32[]{:S(2)}, u32[]{:S(2)}) collective-permute-start(f32[2,256]{1,0:T(2,128)S(1)} %pad_maximum_fusion.5), channel_id=1, source_target_pairs={{0,8},{1,9},{2,10},{3,11},{4,12},{5,13},{6,14},{7,15},{8,0},{9,1},... | collective-permute-start | bytes 6152 | tf_op jit(solution)/shard_map/ppermute | solution.py:47
  91.9 3.7 %collective-permute-start.20 = (f32[256]{0:T(256)S(1)}, f32[256]{0:T(256)S(1)}, u32[]{:S(2)}, u32[]{:S(2)}) collective-permute-start(f32[256]{0:T(256)S(1)} %bitcast.5), channel_id=1, source_target_pairs={{0,2},{1,3},{2,0},{3,1},{4,6},{5,7},{6,4},{7,5},{8,10},{9,11},{10,... | collective-permute-start | bytes 3080 | tf_op jit(solution)/shard_map/ppermute | solution.py:47
